TPU v7x, 256 devices: a whole 4x4x8 slice. The times are simulated.
256 devices in a mesh: seq: 8 (over z), head: 4 (over y_hi, core), rep: 8 (over y_lo, x).
Axes of the slice: x: 4, y: 4 (y_hi: 2, y_lo: 2; y = y_hi * 2 + y_lo), z: 8, core: 2. Of those that a mesh axis runs over, the one named last changes fastest.
Arguments:
- queries: bfloat16 [8, 2048, 7168], P('rep', 'seq', 'head'), may hold values from -6 to 6
- new_keys: bfloat16 [8, 2048, 7168], P('rep', 'seq', 'head'), may hold values from -6 to 6
- new_values: bfloat16 [8, 2048, 7168], P('rep', 'seq', 'head'), may hold values from -4 to 4
- lengths: int32 [8, 4], P('rep'), may hold values from 1 to 1024, 2048 in all within a row
- offsets: int32 [8, 4], P('rep'), may hold values from 0 to 4095
- slot_map: int32 [8, 4], P('rep'), may hold values from 0 to 3, each once within a row
Outputs:
- attended: bfloat16 [8, 2048, 7168], P('rep', 'seq', 'head')
- key_cache: bfloat16 [8, 4, 1024, 7168], P('rep', 'head', None, 'seq')
- value_cache: bfloat16 [8, 4, 1024, 7168], P('rep', 'head', None, 'seq')
Inputs may be any that keep to these rules, and one draw needn't show every extreme that they name: `lengths`: each row sums to 2048; its first entry is the group's shared prompt; every row has one entry equal to 1024. `slot_map`: each row is a permutation of the group's requests.
All inputs are finite; a program needn't handle non-finite values.
Results may differ from a plain program's by a relative error of at most 0.011.
Values may be sent and summed in bfloat16 or wider, within the bound.
A program may use at most 128 MiB of HBM per device.

v0:
```python
import math
import jax
import jax.numpy as jnp
from jax import lax
from jax.sharding import PartitionSpec as P

HD = 224
NEG_FILL = -1e30
ROPE_BASE = 10000.0
KEY_BLOCK = 512


def rotate(source, places):
    full_width = source.shape[-1]
    half_width = full_width // 2
    inverse = jnp.power(
        jnp.float32(ROPE_BASE), -2.0 * jnp.arange(half_width, dtype=jnp.float32) / full_width
    )
    angles = places.astype(jnp.float32)[:, None] * inverse[None, :]
    cosine = jnp.cos(angles)[:, None, :]
    sine_terms = jnp.sin(angles)[:, None, :]
    first_part = source[..., :half_width].astype(jnp.float32)
    second_part = source[..., half_width:].astype(jnp.float32)
    rotated = jnp.concatenate(
        [
            first_part * cosine - second_part * sine_terms,
            second_part * cosine + first_part * sine_terms,
        ],
        axis=-1,
    )
    return rotated.astype(jnp.bfloat16)


def token_request(token_ids, ends_at):
    return jnp.sum((token_ids[:, None] >= ends_at[None, :]).astype(jnp.int32), axis=1)


def lookup_rows(request, lookup):
    matches = request[:, None] == jnp.arange(lookup.shape[0], dtype=jnp.int32)[None, :]
    return jnp.sum(jnp.where(matches, lookup[None, :], 0), axis=1)


def empty_state(head_count, row_count):
    return (
        jnp.full((head_count, row_count), NEG_FILL, jnp.float32),
        jnp.zeros((head_count, row_count), jnp.float32),
        jnp.zeros((head_count, row_count, HD), jnp.float32),
    )


def finish(running):
    row_best, row_total, summed = running
    head_count, row_count, _ = summed.shape
    return (
        (summed / row_total[:, :, None])
        .transpose(1, 0, 2)
        .reshape(row_count, head_count * HD)
        .astype(jnp.bfloat16)
    )


def update(
    running, query_token_rows, query_tok, query_req, key_rows, value_rows, key_start, ends_at
):
    row_count = key_rows.shape[0]
    head_count = query_token_rows.shape[1]
    key_token_index = key_start + jnp.arange(row_count, dtype=jnp.int32)
    key_req = token_request(key_token_index, ends_at)
    same_request = (key_req[None, :] == query_req[:, None]) & (
        key_token_index[None, :] <= query_tok[:, None]
    )
    prompt_keys = (key_req[None, :] == 0) & (query_req[:, None] != 0)
    allowed = same_request | prompt_keys
    row_best, row_total, summed = running
    key_head_stack = key_rows.reshape(row_count, head_count, HD)
    value_heads = value_rows.reshape(row_count, head_count, HD)
    scores = jnp.einsum(
        "ezq,izq->zei", query_token_rows, key_head_stack, preferred_element_type=jnp.float32
    ) * (1.0 / math.sqrt(HD))
    scores = jnp.where(allowed[None], scores, NEG_FILL)
    best_new = jnp.maximum(row_best, jnp.max(scores, axis=2))
    factor = jnp.exp(row_best - best_new)
    weights = jnp.where(allowed[None], jnp.exp(scores - best_new[:, :, None]), 0.0)
    total_new = row_total * factor + jnp.sum(weights, axis=2)
    mixed = jnp.einsum(
        "eva,ael->evl",
        weights.astype(jnp.bfloat16),
        value_heads,
        preferred_element_type=jnp.float32,
    )
    return (best_new, total_new, summed * factor[:, :, None] + mixed)


def per_device(queries, new_keys, new_values, lengths, offsets, slot_map):
    tok_dev = queries.shape[1]
    local_cols = queries.shape[2]
    head_count = local_cols // HD
    tokens_total = tok_dev * lax.axis_size("seq")
    cache_len = tokens_total // 2
    lengths_row = lengths[0]
    offsets_row = offsets[0]
    slots_row = slot_map[0]
    request_count = lengths_row.shape[0]
    ends_at = jnp.cumsum(lengths_row)
    begins = ends_at - lengths_row
    token_ids = lax.axis_index("seq") * tok_dev + jnp.arange(tok_dev, dtype=jnp.int32)
    request = token_request(token_ids, ends_at)
    places = lookup_rows(request, offsets_row) + token_ids - lookup_rows(request, begins)
    rot_queries = rotate(queries[0].reshape(tok_dev, head_count, HD), places)
    rot_keys = rotate(new_keys[0].reshape(tok_dev, head_count, HD), places).reshape(
        tok_dev, local_cols
    )
    value_rows = new_values[0]
    key_rows = lax.all_gather(rot_keys, "seq", axis=0, tiled=True)
    piece_values = lax.all_gather(value_rows, "seq", axis=0, tiled=True)
    row_count = key_rows.shape[0]

    def key_step(key_index, state_in):
        first_row = key_index * KEY_BLOCK
        return update(
            state_in,
            rot_queries,
            token_ids,
            request,
            lax.dynamic_slice_in_dim(key_rows, first_row, KEY_BLOCK, 0),
            lax.dynamic_slice_in_dim(piece_values, first_row, KEY_BLOCK, 0),
            first_row,
            ends_at,
        )

    finished = lax.fori_loop(0, row_count // KEY_BLOCK, key_step, empty_state(head_count, tok_dev))
    attended = finish(finished)
    stacked = jnp.stack([rot_keys, value_rows])
    my_slot = lax.axis_index("head")
    request_ids = jnp.arange(request_count, dtype=jnp.int32)
    owner = jnp.sum(jnp.where(slots_row == my_slot, request_ids, 0))
    owner_begin = jnp.sum(jnp.where(request_ids == owner, begins, 0))
    slot_of = lookup_rows(request, slots_row)
    member = slot_of[None, :] == request_ids[:, None]
    buckets = jnp.where(member[None, :, :, None], stacked[:, None], jnp.zeros((), jnp.bfloat16))
    moved = lax.all_to_all(
        lax.all_to_all(buckets, "head", split_axis=1, concat_axis=3, tiled=True),
        "seq",
        split_axis=3,
        concat_axis=2,
        tiled=True,
    )
    padded = jnp.concatenate(
        [moved, jnp.zeros((2, 1, cache_len, moved.shape[3]), jnp.bfloat16)], axis=2
    )
    window = lax.dynamic_slice_in_dim(padded, owner_begin, cache_len, 2)
    return (attended[None], window[0:1], window[1:2])


def solution(mesh):
    in_specs = (
        P("rep", "seq", "head"),
        P("rep", "seq", "head"),
        P("rep", "seq", "head"),
        P("rep", None),
        P("rep", None),
        P("rep", None),
    )
    out_specs = (
        P("rep", "seq", "head"),
        P("rep", "head", None, "seq"),
        P("rep", "head", None, "seq"),
    )
    return jax.shard_map(
        per_device, mesh=mesh, in_specs=in_specs, out_specs=out_specs, check_vma=False
    )
```

profile of v0, /device:TPU:96, one launch (start us, length us, event | category | flops | bytes accessed | tf_op | source)
XLA Modules:
  0.0 385.8 jit_solution(3452643616625133445)
XLA Ops:
  7.3 0.9 reduce-window.4
  8.1 0.7 fusion.29
  8.8 1.5 copy.46
  10.4 0.8 select_reduce_fusion
  11.1 0.5 multiply_cosine_fusion
  11.6 0.3 fusion.21
  11.9 1.0 maximum_convert_fusion
  13.0 1.3 copy.48
  14.3 0.6 copy.49
  14.9 1.4 pad_maximum_fusion
  16.3 2.8 copy.50
  19.1 3.4 broadcast_select_fusion
  22.6 5.6 %all-to-all-start = ((bf16[2,4,256,1792]{2,3,0,1:T(8,128)(2,1)}), bf16[2,4,256,1792]{2,3,0,1:T(8,128)(2,1)}, u32[]{:S(2)}, u32[]{:S(2)}) async-start(bf16[2,4,256,1792]{2,3,0,1:T(8,128)(2,1)} %broadcast_select_fusion), calls=%async_computation | async-start | bytes 14680064 | tf_op jit(solution)/shard_map/all_to_all | solution.py:142
  28.2 0.5 copy.47
  28.8 0.7 fusion.27
  29.5 1.3 fusion.28
  32.6 0.3 fusion.24
  33.0 78.6 %all-to-all-done = bf16[2,4,256,1792]{2,3,0,1:T(8,128)(2,1)} async-done(((bf16[2,4,256,1792]{2,3,0,1:T(8,128)(2,1)}), bf16[2,4,256,1792]{2,3,0,1:T(8,128)(2,1)}, u32[]{:S(2)}, u32[]{:S(2)}) %all-to-all-start) | async-done | bytes 7340064 | tf_op jit(solution)/shard_map/all_to_all | solution.py:142
  111.6 3.6 copy.51
  115.2 47.2 %copy.52 = bf16[2,1,256,7168]{2,0,1,3:T(2,128)(2,1)} copy(bf16[2,1,256,7168]{2,3,0,1:T(8,128)(2,1)S(1)} %bitcast.73) | data formatting | bytes 14680064 | tf_op jit(solution)/shard_map/all_to_all | solution.py:142
  162.3 7.7 %all-to-all-start.1 = ((bf16[2,1,256,7168]{2,0,1,3:T(2,128)(2,1)}), bf16[2,1,256,7168]{2,0,1,3:T(2,128)(2,1)}, u32[]{:S(2)}, u32[]{:S(2)}) async-start(bf16[2,1,256,7168]{2,0,1,3:T(2,128)(2,1)} %copy.52), calls=%async_computation.1 | async-start | bytes 14680064 | tf_op jit(solution)/shard_map/all_to_all | solution.py:141
  170.0 106.1 %all-gather.6.cloned.1.call-done = bf16[1,2048,1792]{1,2,0:T(8,128)(2,1)} async-done(((bf16[1,256,1792]{1,2,0:T(8,128)(2,1)}), bf16[1,2048,1792]{1,2,0:T(8,128)(2,1)}) %all-gather.6.cloned.1.call-update) | async-done | bytes 7340048 | tf_op jit(solution)/shard_map/all_gather | solution.py:115
  276.2 51.9 %while.18 = (s32[]{:T(128)}, f32[8,256]{1,0:T(8,128)S(1)}, f32[8,256]{1,0:T(8,128)S(1)}, f32[8,256,224]{1,2,0:T(8,128)}, s32[4]{0:T(128)S(1)}, /*index=5*/s32[25...) while((s32[]{:T(128)}, f32[8,256]{1,0:T(8,128)S(1)}, ...), condition=%wide.region_8.9_spmd.clone, body=%wide.region_4.8_spmd.clone.sunk | while | flops 955204608 | bytes 45631228 | solution.py:131
  276.3 0.3 and_or_fusion.2
  276.6 2.3 constant_dynamic-slice_fusion.3
  278.9 3.1 fusion.45
  281.9 3.3 fusion.46
  285.4 2.6 fusion.48
  288.1 0.3 and_or_fusion.2
  288.4 2.3 constant_dynamic-slice_fusion.3
  290.7 3.1 fusion.45
  293.8 3.3 fusion.46
  297.2 4.1 %fusion.48 = f32[8,256,224]{1,2,0:T(8,128)} fusion(f32[8,256,224]{1,2,0:T(8,128)} %get-tuple-element.350, bf16[512,8,224]{0,2,1:T(8,128)(2,1)S(1)} %bitcast.71, f32[8,512,256]{2,1,0:T(8,128)S(1)} %copy-done, f32[8,256]{1,0:T(8,128)S(1)} %select_maximum_fusion.2, pred[256,512]{0,1:T(8,128)(4,1)S(1)} %and_or_fusion.2, ...), kind=kOutput, calls=%fused_computation.13.clone.1 | convolution fusion | flops 476381184 | bytes 9846785 | tf_op jit(solution)/shard_map/while/body/eval_jaxpr/eva,ael->evl/dot_general | solution.py:85
  301.5 0.3 and_or_fusion.2
  301.8 2.3 constant_dynamic-slice_fusion.3
  304.1 3.1 fusion.45
  307.2 3.3 fusion.46
  310.6 4.1 %fusion.48 = f32[8,256,224]{1,2,0:T(8,128)} fusion(f32[8,256,224]{1,2,0:T(8,128)} %get-tuple-element.350, bf16[512,8,224]{0,2,1:T(8,128)(2,1)S(1)} %bitcast.71, f32[8,512,256]{2,1,0:T(8,128)S(1)} %copy-done, f32[8,256]{1,0:T(8,128)S(1)} %select_maximum_fusion.2, pred[256,512]{0,1:T(8,128)(4,1)S(1)} %and_or_fusion.2, ...), kind=kOutput, calls=%fused_computation.13.clone.1 | convolution fusion | flops 476381184 | bytes 9846785 | tf_op jit(solution)/shard_map/while/body/eval_jaxpr/eva,ael->evl/dot_general | solution.py:85
  315.1 2.3 constant_dynamic-slice_fusion.3
  317.4 3.1 fusion.45
  320.5 3.3 fusion.46
  323.9 4.1 %fusion.48 = f32[8,256,224]{1,2,0:T(8,128)} fusion(f32[8,256,224]{1,2,0:T(8,128)} %get-tuple-element.350, bf16[512,8,224]{0,2,1:T(8,128)(2,1)S(1)} %bitcast.71, f32[8,512,256]{2,1,0:T(8,128)S(1)} %copy-done, f32[8,256]{1,0:T(8,128)S(1)} %select_maximum_fusion.2, pred[256,512]{0,1:T(8,128)(4,1)S(1)} %and_or_fusion.2, ...), kind=kOutput, calls=%fused_computation.13.clone.1 | convolution fusion | flops 476381184 | bytes 9846785 | tf_op jit(solution)/shard_map/while/body/eval_jaxpr/eva,ael->evl/dot_general | solution.py:85
  328.1 1.6 divide_convert_fusion
  329.7 1.4 copy.55
  331.1 24.2 %all-to-all-done.1 = bf16[2,1,256,7168]{2,0,1,3:T(2,128)(2,1)} async-done(((bf16[2,1,256,7168]{2,0,1,3:T(2,128)(2,1)}), bf16[2,1,256,7168]{2,0,1,3:T(2,128)(2,1)}, u32[]{:S(2)}, u32[]{:S(2)}) %all-to-all-start.1) | async-done | bytes 7340064 | tf_op jit(solution)/shard_map/all_to_all | solution.py:141
  355.3 7.0 %copy.53 = bf16[2,1,256,7168]{2,3,0,1:T(8,128)(2,1)} copy(bf16[2,1,256,7168]{2,0,1,3:T(2,128)(2,1)} %all-to-all-done.1) | data formatting | bytes 14680064 | tf_op jit(solution)/shard_map/all_to_all | solution.py:141
  362.3 11.1 %copy.54 = bf16[2,1,8,256,896]{4,3,2,0,1:T(8,128)(2,1)} copy(bf16[2,1,8,256,896]{3,4,2,0,1:T(8,128)(2,1)} %bitcast.74) | data formatting | bytes 14680064 | tf_op jit(solution)/shard_map/all_to_all | solution.py:141
  373.4 5.6 %fusion.19 = (bf16[1,1,1024,896]{3,2,1,0:T(8,128)(2,1)}, bf16[1,1,1024,896]{3,2,1,0:T(8,128)(2,1)}) fusion(s32[]{:T(128)S(6)} %add.111, s32[]{:T(128)S(6)} %select_n.53, bf16[2,1,2048,896]{3,2,0,1:T(8,128)(2,1)} %bitcast.75), kind=kLoop, calls=%fused_computation.32 | loop fusion | bytes 11010056
  (65 shorter events, 1.4 us)
Async XLA Ops:
  7.2 5.8 %copy-start.2 = (bf16[1,256,1792]{2,1,0:T(8,128)(2,1)S(1)}, bf16[1,256,1792]{2,1,0:T(8,128)(2,1)}, u32[]{:S(2)}) copy-start(bf16[1,256,1792]{2,1,0:T(8,128)(2,1)} %param.10) | copy-start | bytes 2752516
  7.2 162.8 %all-gather.4.cloned.1.call-start = ((), (), s32[]{:S(2)}) async-start(), calls=%async_computation.2 | async-start | bytes 8257536 | tf_op jit(solution)/shard_map/all_gather | solution.py:114
  12.9 1.4 copy-start.1
  12.9 263.2 %all-gather.6.cloned.1.call-start = ((), (), s32[]{:S(2)}) async-start(), calls=%async_computation.3 | async-start | bytes 8257536 | tf_op jit(solution)/shard_map/all_gather | solution.py:115
  22.6 5.6 %copy-start.3 = (bf16[1,256,1792]{2,1,0:T(8,128)(2,1)S(1)}, bf16[1,256,1792]{2,1,0:T(8,128)(2,1)}, u32[]{:S(2)}) copy-start(bf16[1,256,1792]{2,1,0:T(8,128)(2,1)} %param.8) | copy-start | bytes 2752516
  22.6 6.2 %copy-start.5 = (s32[1,4]{1,0:T(1,128)S(1)}, s32[1,4]{1,0:T(1,128)}, u32[]{:S(2)}) copy-start(s32[1,4]{1,0:T(1,128)} %param.13) | copy-start | bytes 52
  22.6 6.9 %copy-start.4 = (s32[1,4]{1,0:T(1,128)S(1)}, s32[1,4]{1,0:T(1,128)}, u32[]{:S(2)}) copy-start(s32[1,4]{1,0:T(1,128)} %param.11) | copy-start | bytes 52
  22.6 89.0 %all-to-all-start = ((bf16[2,4,256,1792]{2,3,0,1:T(8,128)(2,1)}), bf16[2,4,256,1792]{2,3,0,1:T(8,128)(2,1)}, u32[]{:S(2)}, u32[]{:S(2)}) async-start(bf16[2,4,256,1792]{2,3,0,1:T(8,128)(2,1)} %broadcast_select_fusion), calls=%async_computation | async-start | bytes 14680064 | tf_op jit(solution)/shard_map/all_to_all | solution.py:142
  162.3 192.9 %all-to-all-start.1 = ((bf16[2,1,256,7168]{2,0,1,3:T(2,128)(2,1)}), bf16[2,1,256,7168]{2,0,1,3:T(2,128)(2,1)}, u32[]{:S(2)}, u32[]{:S(2)}) async-start(bf16[2,1,256,7168]{2,0,1,3:T(2,128)(2,1)} %copy.52), calls=%async_computation.1 | async-start | bytes 14680064 | tf_op jit(solution)/shard_map/all_to_all | solution.py:141
  281.9 3.4 copy-start
  293.8 3.4 copy-start
  307.1 3.4 copy-start
  320.5 3.4 copy-start
Sparse Core Ops, SparseCore 0:
  13.1 91.4 all-gather.3
  106.8 169.2 all-gather.5
where the time goes:
time: 387 us; the launch traced here: 386 us
  waiting for transfers between devices  209 us (54%)
  local copies, waits for them, and re-layouts  92 us (24%)
  other arithmetic  28 us (7%)
  matrix products  27.3 us (7%)
  between operations  16.1 us (4%)
  starting transfers between devices  13.3 us (3%)
    all_gather x1, waiting for transfers between devices, per_device(): piece_values = lax.all_gather(value_rows, 'seq', axis=0, tiled=True)  106 us
    all_to_all x1, waiting for transfers between devices, per_device(): lax.all_to_all(buckets, 'head', split_axis=1, concat_axis=3, tiled=True)  78.6 us
    all_to_all x2, local copies, waits for them, and re-layouts, per_device(): lax.all_to_all(buckets, 'head', split_axis=1, concat_axis=3, tiled=True)  50.7 us
    all_to_all x1, waiting for transfers between devices, per_device(): lax.all_to_all(lax.all_to_all(buckets, 'head', split_axis=1, concat_axis=...  24.2 us
    all_to_all x2, local copies, waits for them, and re-layouts, per_device(): lax.all_to_all(lax.all_to_all(buckets, 'head', split_axis=1, concat_axis=...  18.1 us
    dot_general x4, matrix products, update(): jnp.einsum('eva,ael->evl', weights.astype(jnp.bfloat16), value_heads, pre...  15 us
    reduce_sum x4, other arithmetic, update(): total_new = row_total * factor + jnp.sum(weights, axis=2)  13.3 us
    dot_general x4, matrix products, update(): jnp.einsum('ezq,izq->zei', query_token_rows, key_head_stack, preferred_el...  12.3 us
  transfers between devices with their start and end apart: 4, of which 3 were waited for; matrix products, arithmetic and copies ran while one was open for 31% of the time, Pallas kernels for 0%

commit v1 on v0

--- a/solution.py
+++ b/solution.py
@@ -138,12 +138,20 @@
     slot_of = lookup_rows(request, slots_row)
     member = slot_of[None, :] == request_ids[:, None]
     buckets = jnp.where(member[None, :, :, None], stacked[:, None], jnp.zeros((), jnp.bfloat16))
-    moved = lax.all_to_all(
-        lax.all_to_all(buckets, "head", split_axis=1, concat_axis=3, tiled=True),
-        "seq",
-        split_axis=3,
-        concat_axis=2,
-        tiled=True,
+    moved = jnp.concatenate(
+        lax.all_to_all(
+            jnp.stack(
+                jnp.split(
+                    lax.all_to_all(buckets, "head", split_axis=1, concat_axis=3, tiled=True),
+                    lax.axis_size("seq"),
+                    axis=3,
+                )
+            ),
+            "seq",
+            0,
+            0,
+        ),
+        axis=2,
     )
     padded = jnp.concatenate(
         [moved, jnp.zeros((2, 1, cache_len, moved.shape[3]), jnp.bfloat16)], axis=2

time: 387 us -> 405 us (1.047)
  the two profiles are of different devices: /device:TPU:96 before, /device:TPU:50 now
where the time goes in v1:
time: 405 us; the launch traced here: 404 us
  waiting for transfers between devices  262 us (65%)
  local copies, waits for them, and re-layouts  57.2 us (14%)
  matrix products  27.3 us (7%)
  other arithmetic  26.8 us (7%)
  between operations  16 us (4%)
  starting transfers between devices  14.6 us (4%)
    all_gather x1, waiting for transfers between devices, per_device(): piece_values = lax.all_gather(value_rows, 'seq', axis=0, tiled=True)  186 us
    all_to_all x1, waiting for transfers between devices, per_device(): lax.all_to_all(buckets, 'head', split_axis=1, concat_axis=3, tiled=True)  75.5 us
    unnamed x24, local copies, waits for them, and re-layouts  20.9 us
    dot_general x4, matrix products, update(): jnp.einsum('eva,ael->evl', weights.astype(jnp.bfloat16), value_heads, pre...  15 us
    reduce_sum x4, other arithmetic, update(): total_new = row_total * factor + jnp.sum(weights, axis=2)  13.3 us
    another operation x2, local copies, waits for them, and re-layouts, per_device(): jnp.stack(jnp.split(lax.all_to_all(buckets, 'head', split_axis=1, concat_...  12.3 us
    dot_general x4, matrix products, update(): jnp.einsum('ezq,izq->zei', query_token_rows, key_head_stack, preferred_el...  12.3 us
    all_to_all x1, local copies, waits for them, and re-layouts, per_device(): lax.all_to_all(buckets, 'head', split_axis=1, concat_axis=3, tiled=True)  10.1 us
  transfers between devices with their start and end apart: 4, of which 2 were waited for; matrix products, arithmetic and copies ran while one was open for 24% of the time, Pallas kernels for 0%

profile of v1, /device:TPU:50, one launch (start us, length us, event | category | flops | bytes accessed | tf_op | source)
XLA Modules:
  0.0 403.7 jit_solution(6367399967083453207)
XLA Ops:
  7.3 0.9 reduce-window.4
  8.1 0.7 fusion.37
  8.8 1.5 copy.53
  10.4 0.8 select_reduce_fusion
  11.1 0.5 multiply_cosine_fusion
  11.6 0.3 fusion.21
  11.9 1.0 maximum_convert_fusion
  13.0 1.3 copy.55
  14.3 0.6 copy.56
  15.1 3.5 broadcast_select_fusion
  18.6 5.9 %all-to-all-start = ((bf16[2,4,256,1792]{3,2,0,1:T(8,128)(2,1)}), bf16[2,4,256,1792]{3,2,0,1:T(8,128)(2,1)}, u32[]{:S(2)}, u32[]{:S(2)}) async-start(bf16[2,4,256,1792]{3,2,0,1:T(8,128)(2,1)} %broadcast_select_fusion), calls=%async_computation | async-start | bytes 14680064 | tf_op jit(solution)/shard_map/all_to_all | solution.py:145
  24.5 0.5 copy.54
  25.1 0.7 fusion.35
  25.8 1.3 fusion.36
  29.3 75.5 %all-to-all-done = bf16[2,4,256,1792]{3,2,0,1:T(8,128)(2,1)} async-done(((bf16[2,4,256,1792]{3,2,0,1:T(8,128)(2,1)}), bf16[2,4,256,1792]{3,2,0,1:T(8,128)(2,1)}, u32[]{:S(2)}, u32[]{:S(2)}) %all-to-all-start) | async-done | bytes 7340064 | tf_op jit(solution)/shard_map/all_to_all | solution.py:145
  104.9 10.1 %copy.57 = bf16[2,4,256,1792]{2,3,1,0:T(8,128)(2,1)} copy(bf16[2,4,256,1792]{3,2,0,1:T(8,128)(2,1)} %all-to-all-done) | data formatting | bytes 14680064 | tf_op jit(solution)/shard_map/all_to_all | solution.py:145
  114.9 2.3 fusion.34
  117.2 2.5 fusion.33
  119.8 2.2 fusion.32
  122.0 2.3 fusion.31
  124.3 1.1 fusion.30
  125.3 1.0 fusion.29
  126.3 1.0 fusion.28
  127.3 1.0 fusion.27
  128.3 11.3 %copy.58 = bf16[8,2,1,256,896]{4,3,1,2,0:T(8,128)(2,1)} copy(bf16[8,2,1,256,896]{3,4,1,2,0:T(8,128)(2,1)} %fusion.27) | data formatting | bytes 14680064 | tf_op jit(solution)/shard_map/stack | solution.py:143
  139.6 8.6 %all-to-all-start.1 = ((bf16[8,2,1,256,896]{4,3,1,2,0:T(8,128)(2,1)}), bf16[8,2,1,256,896]{4,3,1,2,0:T(8,128)(2,1)}, u32[]{:S(2)}, u32[]{:S(2)}) async-start(bf16[8,2,1,256,896]{4,3,1,2,0:T(8,128)(2,1)} %copy.58), calls=%async_computation.1 | async-start | bytes 14680064 | tf_op jit(solution)/shard_map/all_to_all | solution.py:142
  148.2 186.1 %all-gather.6.cloned.1.call-done = bf16[1,2048,1792]{1,2,0:T(8,128)(2,1)} async-done(((bf16[1,256,1792]{1,2,0:T(8,128)(2,1)}), bf16[1,2048,1792]{1,2,0:T(8,128)(2,1)}) %all-gather.6.cloned.1.call-update) | async-done | bytes 7340048 | tf_op jit(solution)/shard_map/all_gather | solution.py:115
  334.3 51.9 %while.18 = (s32[]{:T(128)}, f32[8,256]{1,0:T(8,128)S(1)}, f32[8,256]{1,0:T(8,128)S(1)}, f32[8,256,224]{1,2,0:T(8,128)}, s32[4]{0:T(128)S(1)}, /*index=5*/s32[25...) while((s32[]{:T(128)}, f32[8,256]{1,0:T(8,128)S(1)}, ...), condition=%wide.region_8.9_spmd.clone, body=%wide.region_4.8_spmd.clone.sunk | while | flops 955204608 | bytes 45631228 | solution.py:131
  334.7 2.3 constant_dynamic-slice_fusion.3
  337.0 3.1 fusion.53
  340.0 3.3 fusion.54
  343.5 2.6 fusion.56
  346.5 2.3 constant_dynamic-slice_fusion.3
  348.8 3.1 fusion.53
  351.9 3.3 fusion.54
  355.3 4.1 %fusion.56 = f32[8,256,224]{1,2,0:T(8,128)} fusion(f32[8,256,224]{1,2,0:T(8,128)} %get-tuple-element.350, bf16[512,8,224]{0,2,1:T(8,128)(2,1)S(1)} %bitcast.102, f32[8,512,256]{2,1,0:T(8,128)S(1)} %copy-done, f32[8,256]{1,0:T(8,128)S(1)} %select_maximum_fusion.2, pred[256,512]{0,1:T(8,128)(4,1)S(1)} %and_or_fusion.2, ...), kind=kOutput, calls=%fused_computation.13.clone.1 | convolution fusion | flops 476381184 | bytes 9846785 | tf_op jit(solution)/shard_map/while/body/eval_jaxpr/eva,ael->evl/dot_general | solution.py:85
  359.9 2.3 constant_dynamic-slice_fusion.3
  362.2 3.1 fusion.53
  365.3 3.3 fusion.54
  368.7 4.1 %fusion.56 = f32[8,256,224]{1,2,0:T(8,128)} fusion(f32[8,256,224]{1,2,0:T(8,128)} %get-tuple-element.350, bf16[512,8,224]{0,2,1:T(8,128)(2,1)S(1)} %bitcast.102, f32[8,512,256]{2,1,0:T(8,128)S(1)} %copy-done, f32[8,256]{1,0:T(8,128)S(1)} %select_maximum_fusion.2, pred[256,512]{0,1:T(8,128)(4,1)S(1)} %and_or_fusion.2, ...), kind=kOutput, calls=%fused_computation.13.clone.1 | convolution fusion | flops 476381184 | bytes 9846785 | tf_op jit(solution)/shard_map/while/body/eval_jaxpr/eva,ael->evl/dot_general | solution.py:85
  373.2 2.3 constant_dynamic-slice_fusion.3
  375.5 3.1 fusion.53
  378.6 3.3 fusion.54
  382.0 4.1 %fusion.56 = f32[8,256,224]{1,2,0:T(8,128)} fusion(f32[8,256,224]{1,2,0:T(8,128)} %get-tuple-element.350, bf16[512,8,224]{0,2,1:T(8,128)(2,1)S(1)} %bitcast.102, f32[8,512,256]{2,1,0:T(8,128)S(1)} %copy-done, f32[8,256]{1,0:T(8,128)S(1)} %select_maximum_fusion.2, pred[256,512]{0,1:T(8,128)(4,1)S(1)} %and_or_fusion.2, ...), kind=kOutput, calls=%fused_computation.13.clone.1 | convolution fusion | flops 476381184 | bytes 9846785 | tf_op jit(solution)/shard_map/while/body/eval_jaxpr/eva,ael->evl/dot_general | solution.py:85
  386.2 1.6 divide_convert_fusion
  387.8 1.4 copy.60
  389.2 3.9 copy.59
  393.1 3.8 fusion.19
  (73 shorter events, 2.7 us)
Async XLA Ops:
  7.2 5.8 %copy-start.3 = (bf16[1,256,1792]{2,1,0:T(8,128)(2,1)S(1)}, bf16[1,256,1792]{2,1,0:T(8,128)(2,1)}, u32[]{:S(2)}) copy-start(bf16[1,256,1792]{2,1,0:T(8,128)(2,1)} %param.10) | copy-start | bytes 2752516
  7.2 141.0 %all-gather.4.cloned.1.call-start = ((), (), s32[]{:S(2)}) async-start(), calls=%async_computation.2 | async-start | bytes 8257536 | tf_op jit(solution)/shard_map/all_gather | solution.py:114
  12.9 1.4 copy-start.2
  12.9 321.3 %all-gather.6.cloned.1.call-start = ((), (), s32[]{:S(2)}) async-start(), calls=%async_computation.3 | async-start | bytes 8257536 | tf_op jit(solution)/shard_map/all_gather | solution.py:115
  18.6 5.9 %copy-start.4 = (bf16[1,256,1792]{2,1,0:T(8,128)(2,1)S(1)}, bf16[1,256,1792]{2,1,0:T(8,128)(2,1)}, u32[]{:S(2)}) copy-start(bf16[1,256,1792]{2,1,0:T(8,128)(2,1)} %param.8) | copy-start | bytes 2752516
  18.6 6.4 %copy-start.6 = (s32[1,4]{1,0:T(1,128)S(1)}, s32[1,4]{1,0:T(1,128)}, u32[]{:S(2)}) copy-start(s32[1,4]{1,0:T(1,128)} %param.13) | copy-start | bytes 52
  18.6 7.2 %copy-start.5 = (s32[1,4]{1,0:T(1,128)S(1)}, s32[1,4]{1,0:T(1,128)}, u32[]{:S(2)}) copy-start(s32[1,4]{1,0:T(1,128)} %param.11) | copy-start | bytes 52
  18.6 86.2 %all-to-all-start = ((bf16[2,4,256,1792]{3,2,0,1:T(8,128)(2,1)}), bf16[2,4,256,1792]{3,2,0,1:T(8,128)(2,1)}, u32[]{:S(2)}, u32[]{:S(2)}) async-start(bf16[2,4,256,1792]{3,2,0,1:T(8,128)(2,1)} %broadcast_select_fusion), calls=%async_computation | async-start | bytes 14680064 | tf_op jit(solution)/shard_map/all_to_all | solution.py:145
  114.9 9.3 %copy-start.1 = (bf16[2,4,256,1792]{2,3,1,0:T(8,128)(2,1)S(1)}, bf16[2,4,256,1792]{2,3,1,0:T(8,128)(2,1)}, u32[]{:S(2)}) copy-start(bf16[2,4,256,1792]{2,3,1,0:T(8,128)(2,1)} %copy.57) | copy-start | bytes 22020100
  139.6 249.6 %all-to-all-start.1 = ((bf16[8,2,1,256,896]{4,3,1,2,0:T(8,128)(2,1)}), bf16[8,2,1,256,896]{4,3,1,2,0:T(8,128)(2,1)}, u32[]{:S(2)}, u32[]{:S(2)}) async-start(bf16[8,2,1,256,896]{4,3,1,2,0:T(8,128)(2,1)} %copy.58), calls=%async_computation.1 | async-start | bytes 14680064 | tf_op jit(solution)/shard_map/all_to_all | solution.py:142
  340.0 3.4 copy-start
  351.9 3.4 copy-start
  365.2 3.4 copy-start
  378.6 3.4 copy-start
Sparse Core Ops, SparseCore 0:
  13.1 92.7 all-gather.3
  108.1 226.1 all-gather.5
